TPU v7x, 32 devices: a whole 2x2x4 slice. The times are simulated.
32 devices in a mesh: cols: 16 (over z, y, x), params: 2 (over core).
Axes of the slice: x: 2, y: 2, z: 4, core: 2. Of those that a mesh axis runs over, the one named last changes fastest.
Arguments:
- concentration: float32 [128, 16384], P(None, ('cols', 'params')), may hold values from 0.2 to 5
- emissions: float32 [128, 16384], P(None, ('cols', 'params')), may hold values from 0 to 1
- rate_table: float32 [8, 16, 16], replicated, may hold values from 0.01 to 0.3
- species_order: int32 [128], replicated, may hold values from 0 to 127, each once
- sensitivity: float32 [4, 128, 32, 4, 128], P('params', None, 'cols'), may hold values from -6 to 6
- source_terms: bfloat16 [4, 128, 32, 4, 128], P('params', None, 'cols'), may hold values from 0 to 2
- courant_x: float32 [32, 4, 128], P('cols'), may hold values from 0.05 to 0.24
- upwind_x: int32 [32, 4, 128], P('cols'), may hold values from 0 to 1
- courant_y: float32 [32, 4, 128], P('cols'), may hold values from 0.05 to 0.24
- upwind_y: int32 [32, 4, 128], P('cols'), may hold values from 0 to 1
Outputs:
- new_concentration: float32 [128, 16384], P(None, ('cols', 'params'))
- new_sensitivity: float32 [4, 128, 32, 4, 128], P('params', None, 'cols')
- sensitivity_burden: float32 [4, 128], P('params')
- species_burden: float32 [128], replicated
Inputs may be any that keep to these rules, and one draw needn't show every extreme that they name: `species_order`: each species appears exactly once. `upwind_x`: 1 means the wind blows toward higher indices through the face. `upwind_y`: 1 means the wind blows toward higher indices through the face.
All inputs are finite; a program needn't handle non-finite values.
Results may differ from a plain program's by a relative error of at most 0.0016.
Values may be sent and summed in bfloat16 or wider, within the bound.
A program may use at most 128 MiB of HBM per device.

v0:
```python
import jax
import jax.numpy as jnp
from jax import lax
from jax.sharding import PartitionSpec as P

SUBSTEPS = 2


def for_sending(value):

    def short(part):
        return part.astype(jnp.bfloat16) if part.dtype == jnp.float32 else part

    return jax.tree.map(short, value)


def passed_along(value, axis, by):
    devices = lax.axis_size(axis)
    pairs = [(i, i + by) for i in range(devices) if 0 <= i + by < devices]
    return lax.ppermute(value, axis, pairs)


def invert_blocks(matrix):
    size = matrix.shape[1]
    positions = jnp.arange(size)

    def eliminate(pivot_index, current):
        pivot = 1.0 / current[:, pivot_index, pivot_index, :]
        pivot_row = current[:, pivot_index, :, :] * pivot[:, None, :]
        pivot_row = jnp.where(
            (positions == pivot_index)[None, :, None], pivot[:, None, :], pivot_row
        )
        column = current[:, :, pivot_index, :]
        updated = current - column[:, :, None, :] * pivot_row[:, None, :, :]
        updated = jnp.where(
            (positions == pivot_index)[None, None, :, None],
            -column[:, :, None, :] * pivot[:, None, None, :],
            updated,
        )
        updated = jnp.where(
            (positions == pivot_index)[None, :, None, None], pivot_row[:, None, :, :], updated
        )
        return updated

    return lax.fori_loop(0, size, eliminate, matrix)


def build_factors(conc_cells, species_order, rate_table):
    block_count, block_width = (rate_table.shape[0], rate_table.shape[1])
    ordered = jnp.take(conc_cells, species_order, axis=0).reshape(block_count, block_width, -1)
    coupling = rate_table[:, :, :, None] * ordered[:, None, :, :]
    row_total = jnp.sum(coupling, axis=2)
    positions = jnp.arange(block_width)
    identity = (positions[:, None] == positions[None, :]).astype(jnp.float32)
    system = identity[None, :, :, None] * (1.0 + row_total)[:, :, None, :] - coupling
    return invert_blocks(system).astype(jnp.bfloat16)


def apply_blocks(factors, values):
    result = jnp.zeros(values.shape, jnp.float32)
    for column_index in range(factors.shape[2]):
        result = (
            result
            + factors[:, :, column_index, :].astype(jnp.float32)[None]
            * values[:, :, column_index, :][:, :, None, :]
        )
    return result


def across_flux(tracer, courant_y, upwind_y):
    before_y = jnp.concatenate([jnp.zeros_like(tracer[..., :1]), tracer[..., :-1]], axis=4)
    lower_y = courant_y * jnp.where(upwind_y == 1, before_y, -tracer)
    upper_y = jnp.concatenate([lower_y[..., 1:], jnp.zeros_like(lower_y[..., :1])], axis=4)
    return lower_y - upper_y


def advect(tracer, courant_x, upwind_x, courant_y, upwind_y):
    left_plane = passed_along(for_sending(tracer[:, :, -1:]), "cols", 1)
    before_x = jnp.concatenate([left_plane, tracer[:, :, :-1]], axis=2)
    lower_x = courant_x * jnp.where(upwind_x == 1, before_x, -tracer)
    right_plane = passed_along(for_sending(lower_x[:, :, :1]), "cols", -1)
    upper_x = jnp.concatenate([lower_x[:, :, 1:], right_plane], axis=2)
    return tracer + lower_x - upper_x + across_flux(tracer, courant_y, upwind_y)


def shards(
    concentration,
    emissions,
    rate_table,
    species_order,
    sensitivity,
    source_terms,
    courant_x,
    upwind_x,
    courant_y,
    upwind_y,
):
    block_count, block_width = (rate_table.shape[0], rate_table.shape[1])
    groups, species = (sensitivity.shape[0], sensitivity.shape[1])
    planes, layers, across = (sensitivity.shape[2], sensitivity.shape[3], sensitivity.shape[4])
    cell_count = planes * layers * across
    inverse = jnp.argsort(species_order)
    own_factors = build_factors(concentration, species_order, rate_table)
    base_side = jnp.take(concentration + emissions, species_order, axis=0).reshape(
        block_count, block_width, -1
    )
    new_base = apply_blocks(own_factors, base_side[None])[0].reshape(species, -1)
    new_concentration = jnp.take(new_base, inverse, axis=0)
    tracer = sensitivity
    for substep in range(SUBSTEPS):
        tracer = advect(tracer, courant_x, upwind_x, courant_y, upwind_y)
    right_side = jnp.take(tracer + source_terms.astype(jnp.float32), species_order, axis=1)
    right_side = right_side.reshape(groups, block_count, block_width, cell_count)
    result = apply_blocks(lax.all_gather(own_factors, "params", axis=3, tiled=True), right_side)
    new_sensitivity = jnp.take(
        result.reshape(groups, species, planes, layers, across), inverse, axis=1
    )
    partial_sens = jnp.sum(new_sensitivity, axis=(2, 3, 4))
    partial_conc = jnp.sum(new_concentration, axis=1)
    total_cells = cell_count * lax.axis_size("cols")
    group_index = lax.axis_index("params")
    row_table = jnp.zeros((groups * lax.axis_size("params"), species), jnp.float32)
    row_table = lax.dynamic_update_slice(row_table, partial_sens, (group_index * groups, 0))
    table_total, conc_total = lax.psum((row_table, partial_conc), ("cols", "params"))
    sens_total = lax.dynamic_slice(table_total, (group_index * groups, 0), (groups, species))
    return (new_concentration, new_sensitivity, sens_total / total_cells, conc_total / total_cells)


def solution(mesh):
    in_specs = (
        P(None, ("cols", "params")),
        P(None, ("cols", "params")),
        P(),
        P(),
        P("params", None, "cols", None, None),
        P("params", None, "cols", None, None),
        P("cols", None, None),
        P("cols", None, None),
        P("cols", None, None),
        P("cols", None, None),
    )
    out_specs = (
        P(None, ("cols", "params")),
        P("params", None, "cols", None, None),
        P("params", None),
        P(),
    )
    return jax.shard_map(shards, mesh=mesh, in_specs=in_specs, out_specs=out_specs, check_vma=False)
```

profile of v0, /device:TPU:0, one launch (start us, length us, event | category | flops | bytes accessed | tf_op | source)
XLA Modules:
  0.0 349.7 jit_solution(16836673207462641334)
XLA Ops:
  11.6 2.5 sort.17
  15.8 2.5 multiply_subtract_fusion
  18.4 151.3 %while.14 = (s32[]{:T(128)}, f32[8,16,16,512]{3,2,1,0:T(8,128)}, s32[]{:T(128)}) while((s32[]{:T(128)}, f32[8,16,16,512]{3,2,1,0:T(8,128)}, s32[]{:T(128)}) %tuple.112), condition=%wide.region_2.4_spmd.clone, body=%wide.region_1.3_spmd.clone.sunk | while | flops 4460562 | bytes 11632757 | solution.py:45
  19.3 2.0 negate_multiply_fusion.2
  22.5 5.3 %select_select_fusion.2 = f32[8,16,16,512]{3,2,1,0:T(8,128)} fusion(f32[8,16,16,512]{3,2,1,0:T(8,128)} %get-tuple-element.200, f32[8,16,512]{2,1,0:T(8,128)S(1)} %get-tuple-element.194, f32[8,16,512]{2,1,0:T(8,128)S(1)} %get-tuple-element.195, f32[8,16,512]{2,1,0:T(8,128)S(1)} %select_bitcast_fusion.5, pred[16]{0:T(512)(128)(4,1)S(1)} %iota_compare_fusion.3), kind=kLoop, calls=%fused_computation.6.clone.1 | loop fusion | flops 4194304 | bytes 9175056 | tf_op jit(solution)/shard_map/while/body/eval_jaxpr/jit(_where)/select_n | solution.py:40
  28.8 2.0 negate_multiply_fusion.2
  31.9 5.3 %select_select_fusion.2 = f32[8,16,16,512]{3,2,1,0:T(8,128)} fusion(f32[8,16,16,512]{3,2,1,0:T(8,128)} %get-tuple-element.200, f32[8,16,512]{2,1,0:T(8,128)S(1)} %get-tuple-element.194, f32[8,16,512]{2,1,0:T(8,128)S(1)} %get-tuple-element.195, f32[8,16,512]{2,1,0:T(8,128)S(1)} %select_bitcast_fusion.5, pred[16]{0:T(512)(128)(4,1)S(1)} %iota_compare_fusion.3), kind=kLoop, calls=%fused_computation.6.clone.1 | loop fusion | flops 4194304 | bytes 9175056 | tf_op jit(solution)/shard_map/while/body/eval_jaxpr/jit(_where)/select_n | solution.py:40
  38.2 2.0 negate_multiply_fusion.2
  41.4 5.3 %select_select_fusion.2 = f32[8,16,16,512]{3,2,1,0:T(8,128)} fusion(f32[8,16,16,512]{3,2,1,0:T(8,128)} %get-tuple-element.200, f32[8,16,512]{2,1,0:T(8,128)S(1)} %get-tuple-element.194, f32[8,16,512]{2,1,0:T(8,128)S(1)} %get-tuple-element.195, f32[8,16,512]{2,1,0:T(8,128)S(1)} %select_bitcast_fusion.5, pred[16]{0:T(512)(128)(4,1)S(1)} %iota_compare_fusion.3), kind=kLoop, calls=%fused_computation.6.clone.1 | loop fusion | flops 4194304 | bytes 9175056 | tf_op jit(solution)/shard_map/while/body/eval_jaxpr/jit(_where)/select_n | solution.py:40
  47.7 2.0 negate_multiply_fusion.2
  50.8 5.3 %select_select_fusion.2 = f32[8,16,16,512]{3,2,1,0:T(8,128)} fusion(f32[8,16,16,512]{3,2,1,0:T(8,128)} %get-tuple-element.200, f32[8,16,512]{2,1,0:T(8,128)S(1)} %get-tuple-element.194, f32[8,16,512]{2,1,0:T(8,128)S(1)} %get-tuple-element.195, f32[8,16,512]{2,1,0:T(8,128)S(1)} %select_bitcast_fusion.5, pred[16]{0:T(512)(128)(4,1)S(1)} %iota_compare_fusion.3), kind=kLoop, calls=%fused_computation.6.clone.1 | loop fusion | flops 4194304 | bytes 9175056 | tf_op jit(solution)/shard_map/while/body/eval_jaxpr/jit(_where)/select_n | solution.py:40
  57.1 2.0 negate_multiply_fusion.2
  60.3 5.3 %select_select_fusion.2 = f32[8,16,16,512]{3,2,1,0:T(8,128)} fusion(f32[8,16,16,512]{3,2,1,0:T(8,128)} %get-tuple-element.200, f32[8,16,512]{2,1,0:T(8,128)S(1)} %get-tuple-element.194, f32[8,16,512]{2,1,0:T(8,128)S(1)} %get-tuple-element.195, f32[8,16,512]{2,1,0:T(8,128)S(1)} %select_bitcast_fusion.5, pred[16]{0:T(512)(128)(4,1)S(1)} %iota_compare_fusion.3), kind=kLoop, calls=%fused_computation.6.clone.1 | loop fusion | flops 4194304 | bytes 9175056 | tf_op jit(solution)/shard_map/while/body/eval_jaxpr/jit(_where)/select_n | solution.py:40
  66.6 2.0 negate_multiply_fusion.2
  69.8 5.3 %select_select_fusion.2 = f32[8,16,16,512]{3,2,1,0:T(8,128)} fusion(f32[8,16,16,512]{3,2,1,0:T(8,128)} %get-tuple-element.200, f32[8,16,512]{2,1,0:T(8,128)S(1)} %get-tuple-element.194, f32[8,16,512]{2,1,0:T(8,128)S(1)} %get-tuple-element.195, f32[8,16,512]{2,1,0:T(8,128)S(1)} %select_bitcast_fusion.5, pred[16]{0:T(512)(128)(4,1)S(1)} %iota_compare_fusion.3), kind=kLoop, calls=%fused_computation.6.clone.1 | loop fusion | flops 4194304 | bytes 9175056 | tf_op jit(solution)/shard_map/while/body/eval_jaxpr/jit(_where)/select_n | solution.py:40
  76.0 2.0 negate_multiply_fusion.2
  79.2 5.3 %select_select_fusion.2 = f32[8,16,16,512]{3,2,1,0:T(8,128)} fusion(f32[8,16,16,512]{3,2,1,0:T(8,128)} %get-tuple-element.200, f32[8,16,512]{2,1,0:T(8,128)S(1)} %get-tuple-element.194, f32[8,16,512]{2,1,0:T(8,128)S(1)} %get-tuple-element.195, f32[8,16,512]{2,1,0:T(8,128)S(1)} %select_bitcast_fusion.5, pred[16]{0:T(512)(128)(4,1)S(1)} %iota_compare_fusion.3), kind=kLoop, calls=%fused_computation.6.clone.1 | loop fusion | flops 4194304 | bytes 9175056 | tf_op jit(solution)/shard_map/while/body/eval_jaxpr/jit(_where)/select_n | solution.py:40
  85.5 2.0 negate_multiply_fusion.2
  88.7 5.3 %select_select_fusion.2 = f32[8,16,16,512]{3,2,1,0:T(8,128)} fusion(f32[8,16,16,512]{3,2,1,0:T(8,128)} %get-tuple-element.200, f32[8,16,512]{2,1,0:T(8,128)S(1)} %get-tuple-element.194, f32[8,16,512]{2,1,0:T(8,128)S(1)} %get-tuple-element.195, f32[8,16,512]{2,1,0:T(8,128)S(1)} %select_bitcast_fusion.5, pred[16]{0:T(512)(128)(4,1)S(1)} %iota_compare_fusion.3), kind=kLoop, calls=%fused_computation.6.clone.1 | loop fusion | flops 4194304 | bytes 9175056 | tf_op jit(solution)/shard_map/while/body/eval_jaxpr/jit(_where)/select_n | solution.py:40
  95.0 2.0 negate_multiply_fusion.2
  98.1 5.3 %select_select_fusion.2 = f32[8,16,16,512]{3,2,1,0:T(8,128)} fusion(f32[8,16,16,512]{3,2,1,0:T(8,128)} %get-tuple-element.200, f32[8,16,512]{2,1,0:T(8,128)S(1)} %get-tuple-element.194, f32[8,16,512]{2,1,0:T(8,128)S(1)} %get-tuple-element.195, f32[8,16,512]{2,1,0:T(8,128)S(1)} %select_bitcast_fusion.5, pred[16]{0:T(512)(128)(4,1)S(1)} %iota_compare_fusion.3), kind=kLoop, calls=%fused_computation.6.clone.1 | loop fusion | flops 4194304 | bytes 9175056 | tf_op jit(solution)/shard_map/while/body/eval_jaxpr/jit(_where)/select_n | solution.py:40
  104.4 2.0 negate_multiply_fusion.2
  107.6 5.3 %select_select_fusion.2 = f32[8,16,16,512]{3,2,1,0:T(8,128)} fusion(f32[8,16,16,512]{3,2,1,0:T(8,128)} %get-tuple-element.200, f32[8,16,512]{2,1,0:T(8,128)S(1)} %get-tuple-element.194, f32[8,16,512]{2,1,0:T(8,128)S(1)} %get-tuple-element.195, f32[8,16,512]{2,1,0:T(8,128)S(1)} %select_bitcast_fusion.5, pred[16]{0:T(512)(128)(4,1)S(1)} %iota_compare_fusion.3), kind=kLoop, calls=%fused_computation.6.clone.1 | loop fusion | flops 4194304 | bytes 9175056 | tf_op jit(solution)/shard_map/while/body/eval_jaxpr/jit(_where)/select_n | solution.py:40
  113.9 2.0 negate_multiply_fusion.2
  117.0 5.3 %select_select_fusion.2 = f32[8,16,16,512]{3,2,1,0:T(8,128)} fusion(f32[8,16,16,512]{3,2,1,0:T(8,128)} %get-tuple-element.200, f32[8,16,512]{2,1,0:T(8,128)S(1)} %get-tuple-element.194, f32[8,16,512]{2,1,0:T(8,128)S(1)} %get-tuple-element.195, f32[8,16,512]{2,1,0:T(8,128)S(1)} %select_bitcast_fusion.5, pred[16]{0:T(512)(128)(4,1)S(1)} %iota_compare_fusion.3), kind=kLoop, calls=%fused_computation.6.clone.1 | loop fusion | flops 4194304 | bytes 9175056 | tf_op jit(solution)/shard_map/while/body/eval_jaxpr/jit(_where)/select_n | solution.py:40
  123.3 2.0 negate_multiply_fusion.2
  126.5 5.3 %select_select_fusion.2 = f32[8,16,16,512]{3,2,1,0:T(8,128)} fusion(f32[8,16,16,512]{3,2,1,0:T(8,128)} %get-tuple-element.200, f32[8,16,512]{2,1,0:T(8,128)S(1)} %get-tuple-element.194, f32[8,16,512]{2,1,0:T(8,128)S(1)} %get-tuple-element.195, f32[8,16,512]{2,1,0:T(8,128)S(1)} %select_bitcast_fusion.5, pred[16]{0:T(512)(128)(4,1)S(1)} %iota_compare_fusion.3), kind=kLoop, calls=%fused_computation.6.clone.1 | loop fusion | flops 4194304 | bytes 9175056 | tf_op jit(solution)/shard_map/while/body/eval_jaxpr/jit(_where)/select_n | solution.py:40
  132.8 2.0 negate_multiply_fusion.2
  135.9 5.3 %select_select_fusion.2 = f32[8,16,16,512]{3,2,1,0:T(8,128)} fusion(f32[8,16,16,512]{3,2,1,0:T(8,128)} %get-tuple-element.200, f32[8,16,512]{2,1,0:T(8,128)S(1)} %get-tuple-element.194, f32[8,16,512]{2,1,0:T(8,128)S(1)} %get-tuple-element.195, f32[8,16,512]{2,1,0:T(8,128)S(1)} %select_bitcast_fusion.5, pred[16]{0:T(512)(128)(4,1)S(1)} %iota_compare_fusion.3), kind=kLoop, calls=%fused_computation.6.clone.1 | loop fusion | flops 4194304 | bytes 9175056 | tf_op jit(solution)/shard_map/while/body/eval_jaxpr/jit(_where)/select_n | solution.py:40
  142.2 2.0 negate_multiply_fusion.2
  145.4 5.3 %select_select_fusion.2 = f32[8,16,16,512]{3,2,1,0:T(8,128)} fusion(f32[8,16,16,512]{3,2,1,0:T(8,128)} %get-tuple-element.200, f32[8,16,512]{2,1,0:T(8,128)S(1)} %get-tuple-element.194, f32[8,16,512]{2,1,0:T(8,128)S(1)} %get-tuple-element.195, f32[8,16,512]{2,1,0:T(8,128)S(1)} %select_bitcast_fusion.5, pred[16]{0:T(512)(128)(4,1)S(1)} %iota_compare_fusion.3), kind=kLoop, calls=%fused_computation.6.clone.1 | loop fusion | flops 4194304 | bytes 9175056 | tf_op jit(solution)/shard_map/while/body/eval_jaxpr/jit(_where)/select_n | solution.py:40
  151.7 2.0 negate_multiply_fusion.2
  154.8 5.3 %select_select_fusion.2 = f32[8,16,16,512]{3,2,1,0:T(8,128)} fusion(f32[8,16,16,512]{3,2,1,0:T(8,128)} %get-tuple-element.200, f32[8,16,512]{2,1,0:T(8,128)S(1)} %get-tuple-element.194, f32[8,16,512]{2,1,0:T(8,128)S(1)} %get-tuple-element.195, f32[8,16,512]{2,1,0:T(8,128)S(1)} %select_bitcast_fusion.5, pred[16]{0:T(512)(128)(4,1)S(1)} %iota_compare_fusion.3), kind=kLoop, calls=%fused_computation.6.clone.1 | loop fusion | flops 4194304 | bytes 9175056 | tf_op jit(solution)/shard_map/while/body/eval_jaxpr/jit(_where)/select_n | solution.py:40
  161.1 2.0 negate_multiply_fusion.2
  164.3 5.3 %select_select_fusion.2 = f32[8,16,16,512]{3,2,1,0:T(8,128)} fusion(f32[8,16,16,512]{3,2,1,0:T(8,128)} %get-tuple-element.200, f32[8,16,512]{2,1,0:T(8,128)S(1)} %get-tuple-element.194, f32[8,16,512]{2,1,0:T(8,128)S(1)} %get-tuple-element.195, f32[8,16,512]{2,1,0:T(8,128)S(1)} %select_bitcast_fusion.5, pred[16]{0:T(512)(128)(4,1)S(1)} %iota_compare_fusion.3), kind=kLoop, calls=%fused_computation.6.clone.1 | loop fusion | flops 4194304 | bytes 9175056 | tf_op jit(solution)/shard_map/while/body/eval_jaxpr/jit(_where)/select_n | solution.py:40
  169.7 3.9 %convert_element_type.318 = bf16[8,16,16,512]{3,2,1,0:T(8,128)(2,1)} convert(f32[8,16,16,512]{3,2,1,0:T(8,128)} %get-tuple-element.71) | non-fusion elementwise | flops 1048576 | bytes 6291456 | tf_op jit(solution)/shard_map/convert_element_type | solution.py:56
  173.7 5.0 %collective-permute-start = (bf16[2,128,1,4,128]{4,3,2,1,0:T(4,128)(2,1)S(1)}, bf16[2,128,1,4,128]{4,3,2,1,0:T(4,128)(2,1)S(1)}, u32[]{:S(2)}, u32[]{:S(2)}) collective-permute-start(bf16[2,128,1,4,128]{4,3,2,1,0:T(4,128)(2,1)S(1)} %slice.447), channel_id=1, source_target_pairs={{0,2},{2,4},{4,6},{6,8},{8,10},{10,12},{12,14},{14,16},{16,18},{18... | collective-permute-start | bytes 786440 | tf_op jit(solution)/shard_map/ppermute | solution.py:20
  178.9 5.4 %collective-permute-done = bf16[2,128,1,4,128]{4,3,2,1,0:T(4,128)(2,1)S(1)} collective-permute-done((bf16[2,128,1,4,128]{4,3,2,1,0:T(4,128)(2,1)S(1)}, bf16[2,128,1,4,128]{4,3,2,1,0:T(4,128)(2,1)S(1)}, u32[]{:S(2)}, u32[]{:S(2)}) %collective-permute-start) | collective-permute-done | bytes 262176 | tf_op jit(solution)/shard_map/ppermute | solution.py:20
  186.7 4.4 %slice_convert_fusion.35 = (f32[8,16,1,512]{3,2,1,0:T(1,128)S(1)}, f32[8,16,1,512]{3,2,1,0:T(1,128)S(1)}, f32[8,16,1,512]{3,2,1,0:T(1,128)S(1)}, f32[8,16,1,512]...) fusion(bf16[8,16,16,512]{3,2,1,0:T(8,128)(2,1)S(1)} %copy-done), kind=kLoop, calls=%fused_computation.66 | loop fusion | flops 1048576 | bytes 6291456 | tf_op jit(solution)/shard_map/convert_element_type | solution.py:64
  191.8 3.4 collective-permute-done.1
  196.1 4.6 %collective-permute-start.2 = (bf16[2,128,1,4,128]{4,3,2,1,0:T(4,128)(2,1)S(1)}, bf16[2,128,1,4,128]{4,3,2,1,0:T(4,128)(2,1)S(1)}, u32[]{:S(2)}, u32[]{:S(2)}) collective-permute-start(bf16[2,128,1,4,128]{4,3,2,1,0:T(4,128)(2,1)S(1)} %slice.445), channel_id=1, source_target_pairs={{0,2},{2,4},{4,6},{6,8},{8,10},{10,12},{12,14},{14,16},{16,18},{18... | collective-permute-start | bytes 786440 | tf_op jit(solution)/shard_map/ppermute | solution.py:20
  201.0 3.5 %collective-permute-done.2 = bf16[2,128,1,4,128]{4,3,2,1,0:T(4,128)(2,1)S(1)} collective-permute-done((bf16[2,128,1,4,128]{4,3,2,1,0:T(4,128)(2,1)S(1)}, bf16[2,128,1,4,128]{4,3,2,1,0:T(4,128)(2,1)S(1)}, u32[]{:S(2)}, u32[]{:S(2)}) %collective-permute-start.2) | collective-permute-done | bytes 262176 | tf_op jit(solution)/shard_map/ppermute | solution.py:20
  224.3 2.8 fusion.7
  232.2 1.9 fusion.6
  234.1 2.6 gather_fusion.3
  269.6 18.6 %slice_convert_fusion.19 = (f32[8,16,1,1024]{3,2,1,0:T(1,128)}, f32[8,16,1,1024]{3,2,1,0:T(1,128)}, f32[8,16,1,1024]{3,2,1,0:T(1,128)}, f32[8,16,1,1024]{3,2,1,0...) fusion(bf16[8,16,16,1024]{3,2,1,0:T(8,128)(2,1)} %all-gather.2., ...), kind=kLoop, calls=%fused_computation.50 | loop fusion | flops 2097152 | bytes 12582912 | tf_op jit(solution)/shard_map/convert_element_type | solution.py:64
  288.3 5.7 %multiply_add_fusion = f32[2,128,1,8,128]{4,3,2,1,0:T(8,128)S(1)} fusion(f32[2,128,1,8,128]{4,3,2,1,0:T(8,128)S(1)} %bitcast.314, f32[2,128,1,8,128]{4,3,2,1,0:T(8,128)S(1)} %bitcast.315, f32[2,128,1,8,128]{4,3,2,1,0:T(8,128)S(1)} %bitcast.316, f32[2,128,1,8,128]{4,3,2,1,0:T(8,128)S(1)} %bitcast.317, f32[2,128,1,8,128]{4,3,2,1,0:T(8,128)S(1)} %bitcast.318, ...), kind=kLoop, calls=%fused_computation.28 | loop fusion | flops 8126464 | bytes 26214400 | tf_op jit(solution)/shard_map/add | solution.py:63
  297.4 44.4 %all-reduce.4 = (f32[4,128]{1,0:T(4,128)S(1)}, f32[128]{0:T(128)S(1)}) all-reduce(f32[4,128]{1,0:T(4,128)S(1)} %constant_dynamic-update-slice_fusion, f32[128]{0:T(128)S(1)} %get-tuple-element.95), channel_id=1, replica_groups=mesh['cols'=16,'params'=2] {'cols','params'}, use_global_device_ids=true, to_apply=%region_5.8 | all-reduce | flops 640 | bytes 5120 | tf_op jit(solution)/shard_map/psum | solution.py:124
  (255 shorter events, 104.8 us)
Async XLA Ops:
  7.2 4.4 %copy-start.21 = (s32[128]{0:T(128)S(1)}, s32[128]{0:T(128)}, u32[]{:S(2)}) copy-start(s32[128]{0:T(128)} %param.19) | copy-start | bytes 1540
  7.2 7.6 %copy-start.12 = (f32[8,16,16]{2,1,0:T(8,128)S(1)}, f32[8,16,16]{2,1,0:T(8,128)}, u32[]{:S(2)}) copy-start(f32[8,16,16]{2,1,0:T(8,128)} %param.18) | copy-start | bytes 24580
  7.2 262.3 %all-gather.2.cloned.1.call-start = ((), (), s32[]{:S(2)}) async-start(), calls=%async_computation | async-start | bytes 6291456 | tf_op jit(solution)/shard_map/all_gather | solution.py:114
  7.9 10.5 %copy-start.15 = (s32[1024]{0:T(1024)}, s32[1024]{0:T(1024)S(1)}, u32[]{:S(2)}) copy-start(s32[1024]{0:T(1024)S(1)} %pad_clamp_fusion.1) | copy-start | bytes 12292
  14.6 3.7 %copy-start.16 = (pred[128]{0:T(512)(128)(4,1)}, pred[128]{0:T(512)(128)(4,1)S(1)}, u32[]{:S(2)}) copy-start(pred[128]{0:T(512)(128)(4,1)S(1)} %get-tuple-element.172) | copy-start | bytes 388
  169.6 4.0 %copy-start.1 = (f32[2,128,2,4,128]{4,3,2,1,0:T(4,128)S(1)}, f32[2,128,2,4,128]{4,3,2,1,0:T(4,128)}, u32[]{:S(2)}) copy-start(f32[2,128,2,4,128]{4,3,2,1,0:T(4,128)} %param.20) | copy-start | bytes 3145732
  169.6 9.2 %copy-start.19 = (s32[2,4,128]{2,1,0:T(4,128)S(1)}, s32[2,4,128]{2,1,0:T(4,128)}, u32[]{:S(2)}) copy-start(s32[2,4,128]{2,1,0:T(4,128)} %param.25) | copy-start | bytes 12292
  169.6 9.2 %copy-start.20 = (s32[2,4,128]{2,1,0:T(4,128)S(1)}, s32[2,4,128]{2,1,0:T(4,128)}, u32[]{:S(2)}) copy-start(s32[2,4,128]{2,1,0:T(4,128)} %param.23) | copy-start | bytes 12292
  169.6 14.7 %copy-start.13 = (f32[2,4,128]{2,1,0:T(4,128)S(1)}, f32[2,4,128]{2,1,0:T(4,128)}, u32[]{:S(2)}) copy-start(f32[2,4,128]{2,1,0:T(4,128)} %param.24) | copy-start | bytes 12292
  169.6 14.7 %copy-start.14 = (f32[2,4,128]{2,1,0:T(4,128)S(1)}, f32[2,4,128]{2,1,0:T(4,128)}, u32[]{:S(2)}) copy-start(f32[2,4,128]{2,1,0:T(4,128)} %param.22) | copy-start | bytes 12292
  173.6 13.0 %copy-start = (bf16[8,16,16,512]{3,2,1,0:T(8,128)(2,1)S(1)}, bf16[8,16,16,512]{3,2,1,0:T(8,128)(2,1)}, u32[]{:S(2)}) copy-start(bf16[8,16,16,512]{3,2,1,0:T(8,128)(2,1)} %convert_element_type.318) | copy-start | bytes 6291460
  173.7 10.6 %collective-permute-start = (bf16[2,128,1,4,128]{4,3,2,1,0:T(4,128)(2,1)S(1)}, bf16[2,128,1,4,128]{4,3,2,1,0:T(4,128)(2,1)S(1)}, u32[]{:S(2)}, u32[]{:S(2)}) collective-permute-start(bf16[2,128,1,4,128]{4,3,2,1,0:T(4,128)(2,1)S(1)} %slice.447), channel_id=1, source_target_pairs={{0,2},{2,4},{4,6},{6,8},{8,10},{10,12},{12,14},{14,16},{16,18},{18... | collective-permute-start | bytes 786440 | tf_op jit(solution)/shard_map/ppermute | solution.py:20
  185.4 9.8 %collective-permute-start.1 = (bf16[2,128,1,4,128]{4,3,2,1,0:T(4,128)(2,1)S(1)}, bf16[2,128,1,4,128]{4,3,2,1,0:T(4,128)(2,1)S(1)}, u32[]{:S(2)}, u32[]{:S(2)}) collective-permute-start(bf16[2,128,1,4,128]{4,3,2,1,0:T(4,128)(2,1)S(1)} %slice.446), channel_id=1, source_target_pairs={{2,0},{4,2},{6,4},{8,6},{10,8},{12,10},{14,12},{16,14},{18,16},{20... | collective-permute-start | bytes 786440 | tf_op jit(solution)/shard_map/ppermute | solution.py:20
  196.1 8.4 %collective-permute-start.2 = (bf16[2,128,1,4,128]{4,3,2,1,0:T(4,128)(2,1)S(1)}, bf16[2,128,1,4,128]{4,3,2,1,0:T(4,128)(2,1)S(1)}, u32[]{:S(2)}, u32[]{:S(2)}) collective-permute-start(bf16[2,128,1,4,128]{4,3,2,1,0:T(4,128)(2,1)S(1)} %slice.445), channel_id=1, source_target_pairs={{0,2},{2,4},{4,6},{6,8},{8,10},{10,12},{12,14},{14,16},{16,18},{18... | collective-permute-start | bytes 786440 | tf_op jit(solution)/shard_map/ppermute | solution.py:20
  206.3 24.9 %collective-permute-start.3 = (bf16[2,128,1,4,128]{4,3,2,1,0:T(4,128)(2,1)}, bf16[2,128,1,4,128]{4,3,2,1,0:T(4,128)(2,1)}, u32[]{:S(2)}, u32[]{:S(2)}) collective-permute-start(bf16[2,128,1,4,128]{4,3,2,1,0:T(4,128)(2,1)} %slice.444), channel_id=1, source_target_pairs={{2,0},{4,2},{6,4},{8,6},{10,8},{12,10},{14,12},{16,14},{18,16},{20... | collective-permute-start | bytes 786440 | tf_op jit(solution)/shard_map/ppermute | solution.py:20
  228.7 3.5 %copy-start.11 = (bf16[2,128,2,4,128]{4,3,2,1,0:T(4,128)(2,1)S(1)}, bf16[2,128,2,4,128]{4,3,2,1,0:T(4,128)(2,1)}, u32[]{:S(2)}) copy-start(bf16[2,128,2,4,128]{4,3,2,1,0:T(4,128)(2,1)} %param.21) | copy-start | bytes 1572868
  232.2 4.5 %copy-start.17 = (pred[128]{0:T(512)(128)(4,1)S(1)}, pred[128]{0:T(512)(128)(4,1)}, u32[]{:S(2)}) copy-start(pred[128]{0:T(512)(128)(4,1)} %copy-done.16) | copy-start | bytes 388
  269.5 18.7 %copy-start.2 = (f32[2,128,2,4,128]{4,3,2,1,0:T(4,128)S(1)}, f32[2,128,2,4,128]{4,3,2,1,0:T(4,128)}, u32[]{:S(2)}) copy-start(f32[2,128,2,4,128]{4,3,2,1,0:T(4,128)} %mul.791) | copy-start | bytes 3145732
  269.5 18.7 %copy-start.3 = (f32[2,128,2,4,128]{4,3,2,1,0:T(4,128)S(1)}, f32[2,128,2,4,128]{4,3,2,1,0:T(4,128)}, u32[]{:S(2)}) copy-start(f32[2,128,2,4,128]{4,3,2,1,0:T(4,128)} %mul.786) | copy-start | bytes 3145732
  269.5 18.7 %copy-start.4 = (f32[2,128,2,4,128]{4,3,2,1,0:T(4,128)S(1)}, f32[2,128,2,4,128]{4,3,2,1,0:T(4,128)}, u32[]{:S(2)}) copy-start(f32[2,128,2,4,128]{4,3,2,1,0:T(4,128)} %mul.781) | copy-start | bytes 3145732
  269.5 18.7 %copy-start.5 = (f32[2,128,2,4,128]{4,3,2,1,0:T(4,128)S(1)}, f32[2,128,2,4,128]{4,3,2,1,0:T(4,128)}, u32[]{:S(2)}) copy-start(f32[2,128,2,4,128]{4,3,2,1,0:T(4,128)} %mul.776) | copy-start | bytes 3145732
  269.5 18.7 %copy-start.6 = (f32[2,128,2,4,128]{4,3,2,1,0:T(4,128)S(1)}, f32[2,128,2,4,128]{4,3,2,1,0:T(4,128)}, u32[]{:S(2)}) copy-start(f32[2,128,2,4,128]{4,3,2,1,0:T(4,128)} %mul.771) | copy-start | bytes 3145732
  269.5 18.7 %copy-start.7 = (f32[2,128,2,4,128]{4,3,2,1,0:T(4,128)S(1)}, f32[2,128,2,4,128]{4,3,2,1,0:T(4,128)}, u32[]{:S(2)}) copy-start(f32[2,128,2,4,128]{4,3,2,1,0:T(4,128)} %mul.766) | copy-start | bytes 3145732
  269.5 18.7 %copy-start.8 = (f32[2,128,2,4,128]{4,3,2,1,0:T(4,128)S(1)}, f32[2,128,2,4,128]{4,3,2,1,0:T(4,128)}, u32[]{:S(2)}) copy-start(f32[2,128,2,4,128]{4,3,2,1,0:T(4,128)} %mul.761) | copy-start | bytes 3145732
  269.5 18.7 %copy-start.9 = (f32[2,128,2,4,128]{4,3,2,1,0:T(4,128)S(1)}, f32[2,128,2,4,128]{4,3,2,1,0:T(4,128)}, u32[]{:S(2)}) copy-start(f32[2,128,2,4,128]{4,3,2,1,0:T(4,128)} %mul.756) | copy-start | bytes 3145732
  269.5 18.7 %copy-start.10 = (f32[2,128,2,4,128]{4,3,2,1,0:T(4,128)S(1)}, f32[2,128,2,4,128]{4,3,2,1,0:T(4,128)}, u32[]{:S(2)}) copy-start(f32[2,128,2,4,128]{4,3,2,1,0:T(4,128)} %mul.751) | copy-start | bytes 3145732
  288.3 7.0 %copy-start.18 = (pred[128]{0:T(512)(128)(4,1)S(1)}, pred[128]{0:T(512)(128)(4,1)}, u32[]{:S(2)}) copy-start(pred[128]{0:T(512)(128)(4,1)} %get-tuple-element.171) | copy-start | bytes 388
Sparse Core Ops, SparseCore 0:
  173.7 16.3 all-gather.1
where the time goes:
time: 352 us; the launch traced here: 350 us
  other arithmetic  204 us (58%)
  local copies, waits for them, and re-layouts  61.1 us (17%)
  blocking collectives  44.4 us (13%)
  between operations  14.8 us (4%)
  starting transfers between devices  12.4 us (4%)
  waiting for transfers between devices  12.3 us (3%)
    select_n x16, other arithmetic, eliminate(): jnp.where((positions == pivot_index)[None, :, None, None], pivot_row[:, N...  85.5 us
    psum x1, blocking collectives, shards(): lax.psum((row_table, partial_conc), ('cols', 'params'))  44.4 us
    mul x16, other arithmetic, eliminate(): -column[:, :, None, :] * pivot[:, None, None, :]  32.7 us
    mul x49, local copies, waits for them, and re-layouts, apply_blocks(): factors[:, :, column_index, :].astype(jnp.float32)[None]  31.5 us
    convert_element_type x2, other arithmetic, apply_blocks(): factors[:, :, column_index, :].astype(jnp.float32)[None]  23.1 us
    unnamed x77, local copies, waits for them, and re-layouts  17.2 us
    broadcast_in_dim x16, other arithmetic, eliminate(): jnp.where((positions == pivot_index)[None, :, None, None], pivot_row[:, N...  16.8 us
    div x16, other arithmetic, eliminate(): pivot = 1.0 / current[:, pivot_index, pivot_index, :]  14.9 us
  transfers between devices with their start and end apart: 5, of which 3 were waited for; matrix products, arithmetic and copies ran while one was open for 20% of the time, Pallas kernels for 0%

commit v1 on v0

--- a/solution.py
+++ b/solution.py
@@ -4,6 +4,11 @@
 from jax.sharding import PartitionSpec as P
 
 SUBSTEPS = 2
+
+
+def one_after_other(array, axis_one, axis_two):
+    inner = lax.psum(array, axis_one)
+    return lax.psum(inner, axis_two)
 
 
 def for_sending(value):
@@ -121,7 +126,7 @@
     group_index = lax.axis_index("params")
     row_table = jnp.zeros((groups * lax.axis_size("params"), species), jnp.float32)
     row_table = lax.dynamic_update_slice(row_table, partial_sens, (group_index * groups, 0))
-    table_total, conc_total = lax.psum((row_table, partial_conc), ("cols", "params"))
+    table_total, conc_total = one_after_other((row_table, partial_conc), "params", "cols")
     sens_total = lax.dynamic_slice(table_total, (group_index * groups, 0), (groups, species))
     return (new_concentration, new_sensitivity, sens_total / total_cells, conc_total / total_cells)
 

time: 352 us -> 356 us (1.011)
  blocking collectives: 44.4 us -> 48 us
    psum x1 -> x2, blocking collectives: 44.4 us -> 48 us  [the longest x1 45.6 us: one_after_other(): return lax.psum(inner, axis_two)]
where the time goes in v1:
time: 356 us; the launch traced here: 353 us
  other arithmetic  204 us (57%)
  local copies, waits for them, and re-layouts  61 us (17%)
  blocking collectives  48 us (13%)
  between operations  14.8 us (4%)
  starting transfers between devices  12.4 us (3%)
  waiting for transfers between devices  12.3 us (3%)
    select_n x16, other arithmetic, eliminate(): jnp.where((positions == pivot_index)[None, :, None, None], pivot_row[:, N...  85.4 us
    psum x1, blocking collectives, one_after_other(): return lax.psum(inner, axis_two)  45.6 us
    mul x16, other arithmetic, eliminate(): -column[:, :, None, :] * pivot[:, None, None, :]  32.7 us
    mul x49, local copies, waits for them, and re-layouts, apply_blocks(): factors[:, :, column_index, :].astype(jnp.float32)[None]  31.5 us
    convert_element_type x2, other arithmetic, apply_blocks(): factors[:, :, column_index, :].astype(jnp.float32)[None]  23.2 us
    unnamed x77, local copies, waits for them, and re-layouts  17.1 us
    broadcast_in_dim x16, other arithmetic, eliminate(): jnp.where((positions == pivot_index)[None, :, None, None], pivot_row[:, N...  16.8 us
    div x16, other arithmetic, eliminate(): pivot = 1.0 / current[:, pivot_index, pivot_index, :]  14.9 us
  transfers between devices with their start and end apart: 5, of which 3 were waited for; matrix products, arithmetic and copies ran while one was open for 20% of the time, Pallas kernels for 0%

profile of v1, /device:TPU:0, one launch (start us, length us, event | category | flops | bytes accessed | tf_op | source)
XLA Modules:
  0.0 353.3 jit_solution(18159750587518300421)
XLA Ops:
  11.6 2.5 sort.17
  15.8 2.5 multiply_subtract_fusion
  18.4 151.1 %while.14 = (s32[]{:T(128)}, f32[8,16,16,512]{3,2,1,0:T(8,128)}, s32[]{:T(128)}) while((s32[]{:T(128)}, f32[8,16,16,512]{3,2,1,0:T(8,128)}, s32[]{:T(128)}) %tuple.112), condition=%wide.region_2.4_spmd.clone, body=%wide.region_1.3_spmd.clone.sunk | while | flops 4460562 | bytes 11632757 | solution.py:50
  19.3 2.0 negate_multiply_fusion.2
  22.5 5.3 %select_select_fusion.2 = f32[8,16,16,512]{3,2,1,0:T(8,128)} fusion(f32[8,16,16,512]{3,2,1,0:T(8,128)} %get-tuple-element.202, f32[8,16,512]{2,1,0:T(8,128)S(1)} %get-tuple-element.196, f32[8,16,512]{2,1,0:T(8,128)S(1)} %get-tuple-element.197, f32[8,16,512]{2,1,0:T(8,128)S(1)} %select_bitcast_fusion.5, pred[16]{0:T(512)(128)(4,1)S(1)} %iota_compare_fusion.3), kind=kLoop, calls=%fused_computation.6.clone.1 | loop fusion | flops 4194304 | bytes 9175056 | tf_op jit(solution)/shard_map/while/body/eval_jaxpr/jit(_where)/select_n | solution.py:45
  28.8 2.0 negate_multiply_fusion.2
  31.9 5.3 %select_select_fusion.2 = f32[8,16,16,512]{3,2,1,0:T(8,128)} fusion(f32[8,16,16,512]{3,2,1,0:T(8,128)} %get-tuple-element.202, f32[8,16,512]{2,1,0:T(8,128)S(1)} %get-tuple-element.196, f32[8,16,512]{2,1,0:T(8,128)S(1)} %get-tuple-element.197, f32[8,16,512]{2,1,0:T(8,128)S(1)} %select_bitcast_fusion.5, pred[16]{0:T(512)(128)(4,1)S(1)} %iota_compare_fusion.3), kind=kLoop, calls=%fused_computation.6.clone.1 | loop fusion | flops 4194304 | bytes 9175056 | tf_op jit(solution)/shard_map/while/body/eval_jaxpr/jit(_where)/select_n | solution.py:45
  38.2 2.0 negate_multiply_fusion.2
  41.4 5.3 %select_select_fusion.2 = f32[8,16,16,512]{3,2,1,0:T(8,128)} fusion(f32[8,16,16,512]{3,2,1,0:T(8,128)} %get-tuple-element.202, f32[8,16,512]{2,1,0:T(8,128)S(1)} %get-tuple-element.196, f32[8,16,512]{2,1,0:T(8,128)S(1)} %get-tuple-element.197, f32[8,16,512]{2,1,0:T(8,128)S(1)} %select_bitcast_fusion.5, pred[16]{0:T(512)(128)(4,1)S(1)} %iota_compare_fusion.3), kind=kLoop, calls=%fused_computation.6.clone.1 | loop fusion | flops 4194304 | bytes 9175056 | tf_op jit(solution)/shard_map/while/body/eval_jaxpr/jit(_where)/select_n | solution.py:45
  47.6 2.0 negate_multiply_fusion.2
  50.8 5.3 %select_select_fusion.2 = f32[8,16,16,512]{3,2,1,0:T(8,128)} fusion(f32[8,16,16,512]{3,2,1,0:T(8,128)} %get-tuple-element.202, f32[8,16,512]{2,1,0:T(8,128)S(1)} %get-tuple-element.196, f32[8,16,512]{2,1,0:T(8,128)S(1)} %get-tuple-element.197, f32[8,16,512]{2,1,0:T(8,128)S(1)} %select_bitcast_fusion.5, pred[16]{0:T(512)(128)(4,1)S(1)} %iota_compare_fusion.3), kind=kLoop, calls=%fused_computation.6.clone.1 | loop fusion | flops 4194304 | bytes 9175056 | tf_op jit(solution)/shard_map/while/body/eval_jaxpr/jit(_where)/select_n | solution.py:45
  57.1 2.0 negate_multiply_fusion.2
  60.3 5.3 %select_select_fusion.2 = f32[8,16,16,512]{3,2,1,0:T(8,128)} fusion(f32[8,16,16,512]{3,2,1,0:T(8,128)} %get-tuple-element.202, f32[8,16,512]{2,1,0:T(8,128)S(1)} %get-tuple-element.196, f32[8,16,512]{2,1,0:T(8,128)S(1)} %get-tuple-element.197, f32[8,16,512]{2,1,0:T(8,128)S(1)} %select_bitcast_fusion.5, pred[16]{0:T(512)(128)(4,1)S(1)} %iota_compare_fusion.3), kind=kLoop, calls=%fused_computation.6.clone.1 | loop fusion | flops 4194304 | bytes 9175056 | tf_op jit(solution)/shard_map/while/body/eval_jaxpr/jit(_where)/select_n | solution.py:45
  66.5 2.0 negate_multiply_fusion.2
  69.7 5.3 %select_select_fusion.2 = f32[8,16,16,512]{3,2,1,0:T(8,128)} fusion(f32[8,16,16,512]{3,2,1,0:T(8,128)} %get-tuple-element.202, f32[8,16,512]{2,1,0:T(8,128)S(1)} %get-tuple-element.196, f32[8,16,512]{2,1,0:T(8,128)S(1)} %get-tuple-element.197, f32[8,16,512]{2,1,0:T(8,128)S(1)} %select_bitcast_fusion.5, pred[16]{0:T(512)(128)(4,1)S(1)} %iota_compare_fusion.3), kind=kLoop, calls=%fused_computation.6.clone.1 | loop fusion | flops 4194304 | bytes 9175056 | tf_op jit(solution)/shard_map/while/body/eval_jaxpr/jit(_where)/select_n | solution.py:45
  76.0 2.0 negate_multiply_fusion.2
  79.1 5.3 %select_select_fusion.2 = f32[8,16,16,512]{3,2,1,0:T(8,128)} fusion(f32[8,16,16,512]{3,2,1,0:T(8,128)} %get-tuple-element.202, f32[8,16,512]{2,1,0:T(8,128)S(1)} %get-tuple-element.196, f32[8,16,512]{2,1,0:T(8,128)S(1)} %get-tuple-element.197, f32[8,16,512]{2,1,0:T(8,128)S(1)} %select_bitcast_fusion.5, pred[16]{0:T(512)(128)(4,1)S(1)} %iota_compare_fusion.3), kind=kLoop, calls=%fused_computation.6.clone.1 | loop fusion | flops 4194304 | bytes 9175056 | tf_op jit(solution)/shard_map/while/body/eval_jaxpr/jit(_where)/select_n | solution.py:45
  85.4 2.0 negate_multiply_fusion.2
  88.6 5.3 %select_select_fusion.2 = f32[8,16,16,512]{3,2,1,0:T(8,128)} fusion(f32[8,16,16,512]{3,2,1,0:T(8,128)} %get-tuple-element.202, f32[8,16,512]{2,1,0:T(8,128)S(1)} %get-tuple-element.196, f32[8,16,512]{2,1,0:T(8,128)S(1)} %get-tuple-element.197, f32[8,16,512]{2,1,0:T(8,128)S(1)} %select_bitcast_fusion.5, pred[16]{0:T(512)(128)(4,1)S(1)} %iota_compare_fusion.3), kind=kLoop, calls=%fused_computation.6.clone.1 | loop fusion | flops 4194304 | bytes 9175056 | tf_op jit(solution)/shard_map/while/body/eval_jaxpr/jit(_where)/select_n | solution.py:45
  94.9 2.0 negate_multiply_fusion.2
  98.0 5.3 %select_select_fusion.2 = f32[8,16,16,512]{3,2,1,0:T(8,128)} fusion(f32[8,16,16,512]{3,2,1,0:T(8,128)} %get-tuple-element.202, f32[8,16,512]{2,1,0:T(8,128)S(1)} %get-tuple-element.196, f32[8,16,512]{2,1,0:T(8,128)S(1)} %get-tuple-element.197, f32[8,16,512]{2,1,0:T(8,128)S(1)} %select_bitcast_fusion.5, pred[16]{0:T(512)(128)(4,1)S(1)} %iota_compare_fusion.3), kind=kLoop, calls=%fused_computation.6.clone.1 | loop fusion | flops 4194304 | bytes 9175056 | tf_op jit(solution)/shard_map/while/body/eval_jaxpr/jit(_where)/select_n | solution.py:45
  104.3 2.0 negate_multiply_fusion.2
  107.5 5.3 %select_select_fusion.2 = f32[8,16,16,512]{3,2,1,0:T(8,128)} fusion(f32[8,16,16,512]{3,2,1,0:T(8,128)} %get-tuple-element.202, f32[8,16,512]{2,1,0:T(8,128)S(1)} %get-tuple-element.196, f32[8,16,512]{2,1,0:T(8,128)S(1)} %get-tuple-element.197, f32[8,16,512]{2,1,0:T(8,128)S(1)} %select_bitcast_fusion.5, pred[16]{0:T(512)(128)(4,1)S(1)} %iota_compare_fusion.3), kind=kLoop, calls=%fused_computation.6.clone.1 | loop fusion | flops 4194304 | bytes 9175056 | tf_op jit(solution)/shard_map/while/body/eval_jaxpr/jit(_where)/select_n | solution.py:45
  113.8 2.0 negate_multiply_fusion.2
  116.9 5.3 %select_select_fusion.2 = f32[8,16,16,512]{3,2,1,0:T(8,128)} fusion(f32[8,16,16,512]{3,2,1,0:T(8,128)} %get-tuple-element.202, f32[8,16,512]{2,1,0:T(8,128)S(1)} %get-tuple-element.196, f32[8,16,512]{2,1,0:T(8,128)S(1)} %get-tuple-element.197, f32[8,16,512]{2,1,0:T(8,128)S(1)} %select_bitcast_fusion.5, pred[16]{0:T(512)(128)(4,1)S(1)} %iota_compare_fusion.3), kind=kLoop, calls=%fused_computation.6.clone.1 | loop fusion | flops 4194304 | bytes 9175056 | tf_op jit(solution)/shard_map/while/body/eval_jaxpr/jit(_where)/select_n | solution.py:45
  123.2 2.0 negate_multiply_fusion.2
  126.4 5.3 %select_select_fusion.2 = f32[8,16,16,512]{3,2,1,0:T(8,128)} fusion(f32[8,16,16,512]{3,2,1,0:T(8,128)} %get-tuple-element.202, f32[8,16,512]{2,1,0:T(8,128)S(1)} %get-tuple-element.196, f32[8,16,512]{2,1,0:T(8,128)S(1)} %get-tuple-element.197, f32[8,16,512]{2,1,0:T(8,128)S(1)} %select_bitcast_fusion.5, pred[16]{0:T(512)(128)(4,1)S(1)} %iota_compare_fusion.3), kind=kLoop, calls=%fused_computation.6.clone.1 | loop fusion | flops 4194304 | bytes 9175056 | tf_op jit(solution)/shard_map/while/body/eval_jaxpr/jit(_where)/select_n | solution.py:45
  132.6 2.0 negate_multiply_fusion.2
  135.8 5.3 %select_select_fusion.2 = f32[8,16,16,512]{3,2,1,0:T(8,128)} fusion(f32[8,16,16,512]{3,2,1,0:T(8,128)} %get-tuple-element.202, f32[8,16,512]{2,1,0:T(8,128)S(1)} %get-tuple-element.196, f32[8,16,512]{2,1,0:T(8,128)S(1)} %get-tuple-element.197, f32[8,16,512]{2,1,0:T(8,128)S(1)} %select_bitcast_fusion.5, pred[16]{0:T(512)(128)(4,1)S(1)} %iota_compare_fusion.3), kind=kLoop, calls=%fused_computation.6.clone.1 | loop fusion | flops 4194304 | bytes 9175056 | tf_op jit(solution)/shard_map/while/body/eval_jaxpr/jit(_where)/select_n | solution.py:45
  142.1 2.0 negate_multiply_fusion.2
  145.3 5.3 %select_select_fusion.2 = f32[8,16,16,512]{3,2,1,0:T(8,128)} fusion(f32[8,16,16,512]{3,2,1,0:T(8,128)} %get-tuple-element.202, f32[8,16,512]{2,1,0:T(8,128)S(1)} %get-tuple-element.196, f32[8,16,512]{2,1,0:T(8,128)S(1)} %get-tuple-element.197, f32[8,16,512]{2,1,0:T(8,128)S(1)} %select_bitcast_fusion.5, pred[16]{0:T(512)(128)(4,1)S(1)} %iota_compare_fusion.3), kind=kLoop, calls=%fused_computation.6.clone.1 | loop fusion | flops 4194304 | bytes 9175056 | tf_op jit(solution)/shard_map/while/body/eval_jaxpr/jit(_where)/select_n | solution.py:45
  151.5 2.0 negate_multiply_fusion.2
  154.7 5.3 %select_select_fusion.2 = f32[8,16,16,512]{3,2,1,0:T(8,128)} fusion(f32[8,16,16,512]{3,2,1,0:T(8,128)} %get-tuple-element.202, f32[8,16,512]{2,1,0:T(8,128)S(1)} %get-tuple-element.196, f32[8,16,512]{2,1,0:T(8,128)S(1)} %get-tuple-element.197, f32[8,16,512]{2,1,0:T(8,128)S(1)} %select_bitcast_fusion.5, pred[16]{0:T(512)(128)(4,1)S(1)} %iota_compare_fusion.3), kind=kLoop, calls=%fused_computation.6.clone.1 | loop fusion | flops 4194304 | bytes 9175056 | tf_op jit(solution)/shard_map/while/body/eval_jaxpr/jit(_where)/select_n | solution.py:45
  161.0 2.0 negate_multiply_fusion.2
  164.1 5.3 %select_select_fusion.2 = f32[8,16,16,512]{3,2,1,0:T(8,128)} fusion(f32[8,16,16,512]{3,2,1,0:T(8,128)} %get-tuple-element.202, f32[8,16,512]{2,1,0:T(8,128)S(1)} %get-tuple-element.196, f32[8,16,512]{2,1,0:T(8,128)S(1)} %get-tuple-element.197, f32[8,16,512]{2,1,0:T(8,128)S(1)} %select_bitcast_fusion.5, pred[16]{0:T(512)(128)(4,1)S(1)} %iota_compare_fusion.3), kind=kLoop, calls=%fused_computation.6.clone.1 | loop fusion | flops 4194304 | bytes 9175056 | tf_op jit(solution)/shard_map/while/body/eval_jaxpr/jit(_where)/select_n | solution.py:45
  169.5 4.0 %convert_element_type.318 = bf16[8,16,16,512]{3,2,1,0:T(8,128)(2,1)} convert(f32[8,16,16,512]{3,2,1,0:T(8,128)} %get-tuple-element.71) | non-fusion elementwise | flops 1048576 | bytes 6291456 | tf_op jit(solution)/shard_map/convert_element_type | solution.py:61
  173.6 5.0 %collective-permute-start = (bf16[2,128,1,4,128]{4,3,2,1,0:T(4,128)(2,1)S(1)}, bf16[2,128,1,4,128]{4,3,2,1,0:T(4,128)(2,1)S(1)}, u32[]{:S(2)}, u32[]{:S(2)}) collective-permute-start(bf16[2,128,1,4,128]{4,3,2,1,0:T(4,128)(2,1)S(1)} %slice.447), channel_id=1, source_target_pairs={{0,2},{2,4},{4,6},{6,8},{8,10},{10,12},{12,14},{14,16},{16,18},{18... | collective-permute-start | bytes 786440 | tf_op jit(solution)/shard_map/ppermute | solution.py:25
  178.8 5.4 %collective-permute-done = bf16[2,128,1,4,128]{4,3,2,1,0:T(4,128)(2,1)S(1)} collective-permute-done((bf16[2,128,1,4,128]{4,3,2,1,0:T(4,128)(2,1)S(1)}, bf16[2,128,1,4,128]{4,3,2,1,0:T(4,128)(2,1)S(1)}, u32[]{:S(2)}, u32[]{:S(2)}) %collective-permute-start) | collective-permute-done | bytes 262176 | tf_op jit(solution)/shard_map/ppermute | solution.py:25
  186.5 4.4 %slice_convert_fusion.35 = (f32[8,16,1,512]{3,2,1,0:T(1,128)S(1)}, f32[8,16,1,512]{3,2,1,0:T(1,128)S(1)}, f32[8,16,1,512]{3,2,1,0:T(1,128)S(1)}, f32[8,16,1,512]...) fusion(bf16[8,16,16,512]{3,2,1,0:T(8,128)(2,1)S(1)} %copy-done), kind=kLoop, calls=%fused_computation.66 | loop fusion | flops 1048576 | bytes 6291456 | tf_op jit(solution)/shard_map/convert_element_type | solution.py:69
  191.7 3.4 collective-permute-done.1
  195.9 4.6 %collective-permute-start.2 = (bf16[2,128,1,4,128]{4,3,2,1,0:T(4,128)(2,1)S(1)}, bf16[2,128,1,4,128]{4,3,2,1,0:T(4,128)(2,1)S(1)}, u32[]{:S(2)}, u32[]{:S(2)}) collective-permute-start(bf16[2,128,1,4,128]{4,3,2,1,0:T(4,128)(2,1)S(1)} %slice.445), channel_id=1, source_target_pairs={{0,2},{2,4},{4,6},{6,8},{8,10},{10,12},{12,14},{14,16},{16,18},{18... | collective-permute-start | bytes 786440 | tf_op jit(solution)/shard_map/ppermute | solution.py:25
  200.9 3.5 collective-permute-done.2
  224.2 2.8 fusion.7
  234.0 2.6 gather_fusion.3
  269.3 18.8 %slice_convert_fusion.19 = (f32[8,16,1,1024]{3,2,1,0:T(1,128)}, f32[8,16,1,1024]{3,2,1,0:T(1,128)}, f32[8,16,1,1024]{3,2,1,0:T(1,128)}, f32[8,16,1,1024]{3,2,1,0...) fusion(bf16[8,16,16,1024]{3,2,1,0:T(8,128)(2,1)} %all-gather.2., ...), kind=kLoop, calls=%fused_computation.50 | loop fusion | flops 2097152 | bytes 12582912 | tf_op jit(solution)/shard_map/convert_element_type | solution.py:69
  288.3 5.7 %multiply_add_fusion = f32[2,128,1,8,128]{4,3,2,1,0:T(8,128)S(1)} fusion(f32[2,128,1,8,128]{4,3,2,1,0:T(8,128)S(1)} %bitcast.314, f32[2,128,1,8,128]{4,3,2,1,0:T(8,128)S(1)} %bitcast.315, f32[2,128,1,8,128]{4,3,2,1,0:T(8,128)S(1)} %bitcast.316, f32[2,128,1,8,128]{4,3,2,1,0:T(8,128)S(1)} %bitcast.317, f32[2,128,1,8,128]{4,3,2,1,0:T(8,128)S(1)} %bitcast.318, ...), kind=kLoop, calls=%fused_computation.28 | loop fusion | flops 8126464 | bytes 26214400 | tf_op jit(solution)/shard_map/add | solution.py:68
  297.3 2.5 all-reduce.5
  299.8 45.6 %all-reduce.4 = (f32[4,128]{1,0:T(4,128)S(1)}, f32[128]{0:T(128)S(1)}) all-reduce(f32[4,128]{1,0:T(4,128)S(1)} %get-tuple-element.93, f32[128]{0:T(128)S(1)} %get-tuple-element.94), channel_id=1, replica_groups=mesh['cols'=16,'params'=2] {'cols'}, use_global_device_ids=true, to_apply=%region_6.9 | all-reduce | flops 640 | bytes 5120 | tf_op jit(solution)/shard_map/psum | solution.py:11
  (256 shorter events, 106.7 us)
Async XLA Ops:
  7.2 4.4 %copy-start.21 = (s32[128]{0:T(128)S(1)}, s32[128]{0:T(128)}, u32[]{:S(2)}) copy-start(s32[128]{0:T(128)} %param.19) | copy-start | bytes 1540
  7.2 7.6 %copy-start.12 = (f32[8,16,16]{2,1,0:T(8,128)S(1)}, f32[8,16,16]{2,1,0:T(8,128)}, u32[]{:S(2)}) copy-start(f32[8,16,16]{2,1,0:T(8,128)} %param.18) | copy-start | bytes 24580
  7.2 262.1 %all-gather.2.cloned.1.call-start = ((), (), s32[]{:S(2)}) async-start(), calls=%async_computation | async-start | bytes 6291456 | tf_op jit(solution)/shard_map/all_gather | solution.py:119
  7.9 10.5 %copy-start.15 = (s32[1024]{0:T(1024)}, s32[1024]{0:T(1024)S(1)}, u32[]{:S(2)}) copy-start(s32[1024]{0:T(1024)S(1)} %pad_clamp_fusion.1) | copy-start | bytes 12292
  14.6 3.7 %copy-start.16 = (pred[128]{0:T(512)(128)(4,1)}, pred[128]{0:T(512)(128)(4,1)S(1)}, u32[]{:S(2)}) copy-start(pred[128]{0:T(512)(128)(4,1)S(1)} %get-tuple-element.174) | copy-start | bytes 388
  169.5 4.0 %copy-start.1 = (f32[2,128,2,4,128]{4,3,2,1,0:T(4,128)S(1)}, f32[2,128,2,4,128]{4,3,2,1,0:T(4,128)}, u32[]{:S(2)}) copy-start(f32[2,128,2,4,128]{4,3,2,1,0:T(4,128)} %param.20) | copy-start | bytes 3145732
  169.5 9.2 %copy-start.19 = (s32[2,4,128]{2,1,0:T(4,128)S(1)}, s32[2,4,128]{2,1,0:T(4,128)}, u32[]{:S(2)}) copy-start(s32[2,4,128]{2,1,0:T(4,128)} %param.25) | copy-start | bytes 12292
  169.5 9.3 %copy-start.20 = (s32[2,4,128]{2,1,0:T(4,128)S(1)}, s32[2,4,128]{2,1,0:T(4,128)}, u32[]{:S(2)}) copy-start(s32[2,4,128]{2,1,0:T(4,128)} %param.23) | copy-start | bytes 12292
  169.5 14.7 %copy-start.13 = (f32[2,4,128]{2,1,0:T(4,128)S(1)}, f32[2,4,128]{2,1,0:T(4,128)}, u32[]{:S(2)}) copy-start(f32[2,4,128]{2,1,0:T(4,128)} %param.24) | copy-start | bytes 12292
  169.5 14.7 %copy-start.14 = (f32[2,4,128]{2,1,0:T(4,128)S(1)}, f32[2,4,128]{2,1,0:T(4,128)}, u32[]{:S(2)}) copy-start(f32[2,4,128]{2,1,0:T(4,128)} %param.22) | copy-start | bytes 12292
  173.5 13.0 %copy-start = (bf16[8,16,16,512]{3,2,1,0:T(8,128)(2,1)S(1)}, bf16[8,16,16,512]{3,2,1,0:T(8,128)(2,1)}, u32[]{:S(2)}) copy-start(bf16[8,16,16,512]{3,2,1,0:T(8,128)(2,1)} %convert_element_type.318) | copy-start | bytes 6291460
  173.6 10.6 %collective-permute-start = (bf16[2,128,1,4,128]{4,3,2,1,0:T(4,128)(2,1)S(1)}, bf16[2,128,1,4,128]{4,3,2,1,0:T(4,128)(2,1)S(1)}, u32[]{:S(2)}, u32[]{:S(2)}) collective-permute-start(bf16[2,128,1,4,128]{4,3,2,1,0:T(4,128)(2,1)S(1)} %slice.447), channel_id=1, source_target_pairs={{0,2},{2,4},{4,6},{6,8},{8,10},{10,12},{12,14},{14,16},{16,18},{18... | collective-permute-start | bytes 786440 | tf_op jit(solution)/shard_map/ppermute | solution.py:25
  185.2 9.8 %collective-permute-start.1 = (bf16[2,128,1,4,128]{4,3,2,1,0:T(4,128)(2,1)S(1)}, bf16[2,128,1,4,128]{4,3,2,1,0:T(4,128)(2,1)S(1)}, u32[]{:S(2)}, u32[]{:S(2)}) collective-permute-start(bf16[2,128,1,4,128]{4,3,2,1,0:T(4,128)(2,1)S(1)} %slice.446), channel_id=1, source_target_pairs={{2,0},{4,2},{6,4},{8,6},{10,8},{12,10},{14,12},{16,14},{18,16},{20... | collective-permute-start | bytes 786440 | tf_op jit(solution)/shard_map/ppermute | solution.py:25
  195.9 8.4 %collective-permute-start.2 = (bf16[2,128,1,4,128]{4,3,2,1,0:T(4,128)(2,1)S(1)}, bf16[2,128,1,4,128]{4,3,2,1,0:T(4,128)(2,1)S(1)}, u32[]{:S(2)}, u32[]{:S(2)}) collective-permute-start(bf16[2,128,1,4,128]{4,3,2,1,0:T(4,128)(2,1)S(1)} %slice.445), channel_id=1, source_target_pairs={{0,2},{2,4},{4,6},{6,8},{8,10},{10,12},{12,14},{14,16},{16,18},{18... | collective-permute-start | bytes 786440 | tf_op jit(solution)/shard_map/ppermute | solution.py:25
  206.1 24.9 %collective-permute-start.3 = (bf16[2,128,1,4,128]{4,3,2,1,0:T(4,128)(2,1)}, bf16[2,128,1,4,128]{4,3,2,1,0:T(4,128)(2,1)}, u32[]{:S(2)}, u32[]{:S(2)}) collective-permute-start(bf16[2,128,1,4,128]{4,3,2,1,0:T(4,128)(2,1)} %slice.444), channel_id=1, source_target_pairs={{2,0},{4,2},{6,4},{8,6},{10,8},{12,10},{14,12},{16,14},{18,16},{20... | collective-permute-start | bytes 786440 | tf_op jit(solution)/shard_map/ppermute | solution.py:25
  228.5 3.5 copy-start.11
  232.0 4.5 %copy-start.17 = (pred[128]{0:T(512)(128)(4,1)S(1)}, pred[128]{0:T(512)(128)(4,1)}, u32[]{:S(2)}) copy-start(pred[128]{0:T(512)(128)(4,1)} %copy-done.16) | copy-start | bytes 388
  269.3 18.9 %copy-start.2 = (f32[2,128,2,4,128]{4,3,2,1,0:T(4,128)S(1)}, f32[2,128,2,4,128]{4,3,2,1,0:T(4,128)}, u32[]{:S(2)}) copy-start(f32[2,128,2,4,128]{4,3,2,1,0:T(4,128)} %mul.791) | copy-start | bytes 3145732
  269.3 18.9 %copy-start.3 = (f32[2,128,2,4,128]{4,3,2,1,0:T(4,128)S(1)}, f32[2,128,2,4,128]{4,3,2,1,0:T(4,128)}, u32[]{:S(2)}) copy-start(f32[2,128,2,4,128]{4,3,2,1,0:T(4,128)} %mul.786) | copy-start | bytes 3145732
  269.3 18.9 %copy-start.4 = (f32[2,128,2,4,128]{4,3,2,1,0:T(4,128)S(1)}, f32[2,128,2,4,128]{4,3,2,1,0:T(4,128)}, u32[]{:S(2)}) copy-start(f32[2,128,2,4,128]{4,3,2,1,0:T(4,128)} %mul.781) | copy-start | bytes 3145732
  269.3 18.9 %copy-start.5 = (f32[2,128,2,4,128]{4,3,2,1,0:T(4,128)S(1)}, f32[2,128,2,4,128]{4,3,2,1,0:T(4,128)}, u32[]{:S(2)}) copy-start(f32[2,128,2,4,128]{4,3,2,1,0:T(4,128)} %mul.776) | copy-start | bytes 3145732
  269.3 18.9 %copy-start.6 = (f32[2,128,2,4,128]{4,3,2,1,0:T(4,128)S(1)}, f32[2,128,2,4,128]{4,3,2,1,0:T(4,128)}, u32[]{:S(2)}) copy-start(f32[2,128,2,4,128]{4,3,2,1,0:T(4,128)} %mul.771) | copy-start | bytes 3145732
  269.3 18.9 %copy-start.7 = (f32[2,128,2,4,128]{4,3,2,1,0:T(4,128)S(1)}, f32[2,128,2,4,128]{4,3,2,1,0:T(4,128)}, u32[]{:S(2)}) copy-start(f32[2,128,2,4,128]{4,3,2,1,0:T(4,128)} %mul.766) | copy-start | bytes 3145732
  269.3 18.9 %copy-start.8 = (f32[2,128,2,4,128]{4,3,2,1,0:T(4,128)S(1)}, f32[2,128,2,4,128]{4,3,2,1,0:T(4,128)}, u32[]{:S(2)}) copy-start(f32[2,128,2,4,128]{4,3,2,1,0:T(4,128)} %mul.761) | copy-start | bytes 3145732
  269.3 18.9 %copy-start.9 = (f32[2,128,2,4,128]{4,3,2,1,0:T(4,128)S(1)}, f32[2,128,2,4,128]{4,3,2,1,0:T(4,128)}, u32[]{:S(2)}) copy-start(f32[2,128,2,4,128]{4,3,2,1,0:T(4,128)} %mul.756) | copy-start | bytes 3145732
  269.3 18.9 %copy-start.10 = (f32[2,128,2,4,128]{4,3,2,1,0:T(4,128)S(1)}, f32[2,128,2,4,128]{4,3,2,1,0:T(4,128)}, u32[]{:S(2)}) copy-start(f32[2,128,2,4,128]{4,3,2,1,0:T(4,128)} %mul.751) | copy-start | bytes 3145732
  288.2 7.0 %copy-start.18 = (pred[128]{0:T(512)(128)(4,1)S(1)}, pred[128]{0:T(512)(128)(4,1)}, u32[]{:S(2)}) copy-start(pred[128]{0:T(512)(128)(4,1)} %get-tuple-element.173) | copy-start | bytes 388
Sparse Core Ops, SparseCore 0:
  173.6 16.3 all-gather.1
